TPU v7x, 32 devices: a whole 2x2x4 slice. The times are simulated.
32 devices in a mesh: dp: 4 (over y, x), expert: 8 (over z, core).
Axes of the slice: x: 2, y: 2, z: 4, core: 2. Of those that a mesh axis runs over, the one named last changes fastest.
Arguments:
- tokens: bfloat16 [4096, 2048], P(('dp', 'expert')), may hold values from -6 to 6
- out_grad: bfloat16 [4096, 2048], P(('dp', 'expert')), may hold values from -6 to 6
- routes: int32 [4096, 4], P(('dp', 'expert')), may hold values from 0 to 7, all different within a row; in each aligned block of 128 rows (0 to 127, 128 to 255, ...) at most 72 rows name the same one
- gate_values: float32 [4096, 4], P(('dp', 'expert')), may hold values from 0.05 to 1
- w_gate: bfloat16 [8, 2048, 768], P('expert', 'dp'), may hold values from -0.125 to 0.125
- w_up: bfloat16 [8, 2048, 768], P('expert', 'dp'), may hold values from -0.125 to 0.125
- w_down: bfloat16 [8, 768, 2048], P('expert', None, 'dp'), may hold values from -0.21875 to 0.21875
Outputs:
- input_grad: bfloat16 [4096, 2048], P(('dp', 'expert'))
- gate_grad: bfloat16 [8, 2048, 768], P('expert', 'dp')
- up_grad: bfloat16 [8, 2048, 768], P('expert', 'dp')
- down_grad: bfloat16 [8, 768, 2048], P('expert', None, 'dp')
Inputs may be any that keep to these rules, and one draw needn't show every extreme that they name: `routes`: each token names 4 different experts. Among the 128 tokens of one device (aligned blocks of 128 tokens) no expert is named by more than 72 tokens, and in every draw some device names some expert exactly 72 times.
All inputs are finite; a program needn't handle non-finite values.
Results may differ from a plain program's by a relative error of at most 0.0095.
Values may be sent and summed in bfloat16 or wider, within the bound.
No kernel may reach another device: no remote copies, remote signals or barrier semaphores. Data moves between devices by JAX's collectives and lax.ppermute only.
A program may use at most 128 MiB of HBM per device.

v0:
```python
import jax
import jax.numpy as jnp
from jax import lax
from jax.sharding import PartitionSpec as P


def local(tokens, out_grad, routes, gate_values, w_gate, w_up, w_down):
    tok_rows, model_width = tokens.shape
    top_count = routes.shape[1]
    group_count = lax.axis_size("expert")
    local_count = w_gate.shape[0]
    expert_count = group_count * local_count
    hidden_units = w_gate.shape[2]
    capacity = min(tok_rows, max(2, 9 * tok_rows * top_count // (8 * expert_count)))
    pair_count = tok_rows * top_count
    slot_count = group_count * capacity
    expert_of = routes.reshape(-1)
    onehot = (expert_of[:, None] == jnp.arange(expert_count, dtype=jnp.int32)[None, :]).astype(
        jnp.int32
    )
    before = jnp.cumsum(onehot, axis=0) - onehot
    placed = jnp.sum(before * onehot, axis=1)
    slot_of = expert_of * capacity + placed
    slot_table = jnp.full((expert_count * capacity,), pair_count, jnp.int32)
    slot_table = slot_table.at[slot_of].set(jnp.arange(pair_count, dtype=jnp.int32))
    filled = slot_table < pair_count
    source = jnp.where(filled, slot_table, 0)
    owner_row = source // top_count
    send_x = jnp.where(filled[:, None], tokens[owner_row], jnp.zeros((), jnp.bfloat16))
    scaled = gate_values.reshape(-1)[source][:, None] * out_grad[owner_row].astype(jnp.float32)
    send_dy = jnp.where(filled[:, None], scaled, 0.0).astype(jnp.bfloat16)
    send_x = send_x.reshape(expert_count, capacity, model_width)
    send_dy = send_dy.reshape(expert_count, capacity, model_width)
    recv_x, recv_dy = (
        lax.all_to_all(send_x, "expert", split_axis=0, concat_axis=0, tiled=True),
        lax.all_to_all(send_dy, "expert", split_axis=0, concat_axis=0, tiled=True),
    )

    def to_local(stacked):
        shaped = stacked.reshape(group_count, local_count, capacity, model_width)
        return shaped.transpose(1, 0, 2, 3).reshape(local_count, slot_count, model_width)

    slot_x = to_local(recv_x)
    slot_dy = to_local(recv_dy)
    part_x = slot_x
    gate_term = jnp.einsum(
        "asd,adf->asf",
        part_x,
        lax.all_gather(w_gate, "dp", axis=1, tiled=True),
        preferred_element_type=jnp.float32,
    )
    up_term = jnp.einsum(
        "asd,adf->asf",
        part_x,
        lax.all_gather(w_up, "dp", axis=1, tiled=True),
        preferred_element_type=jnp.float32,
    )
    full_gate, full_up, full_down = (
        lax.all_gather(w_gate, "dp", axis=1, tiled=True),
        lax.all_gather(w_up, "dp", axis=1, tiled=True),
        lax.all_gather(w_down, "dp", axis=2, tiled=True),
    )
    sigma = jax.nn.sigmoid(gate_term)
    active = gate_term * sigma
    activated = (active * up_term).astype(jnp.bfloat16)
    back_hidden = jnp.einsum("asd,afd->asf", slot_dy, full_down, preferred_element_type=jnp.float32)
    up_delta = (back_hidden * active).astype(jnp.bfloat16)
    gate_delta = (back_hidden * up_term * sigma * (1.0 + gate_term * (1.0 - sigma))).astype(
        jnp.bfloat16
    )
    pair_grad = (
        jnp.einsum("asf,adf->asd", gate_delta, full_gate, preferred_element_type=jnp.float32)
        + jnp.einsum("asf,adf->asd", up_delta, full_up, preferred_element_type=jnp.float32)
    ).astype(jnp.bfloat16)
    send_back = pair_grad.reshape(local_count, group_count, capacity, model_width).transpose(
        1, 0, 2, 3
    )
    send_back = send_back.reshape(expert_count, capacity, model_width)
    returned = lax.all_to_all(send_back, "expert", split_axis=0, concat_axis=0, tiled=True)
    per_pair = returned.reshape(expert_count * capacity, model_width)[slot_of].astype(jnp.float32)
    input_grad = jnp.sum(per_pair.reshape(tok_rows, top_count, model_width), axis=1).astype(
        jnp.bfloat16
    )
    block_width = local_count * hidden_units
    share_width = model_width // lax.axis_size("dp")
    part_x = slot_x
    term_gate = jnp.einsum("asd,asf->daf", part_x, gate_delta, preferred_element_type=jnp.float32)
    term_up = jnp.einsum("asd,asf->daf", part_x, up_delta, preferred_element_type=jnp.float32)
    term_down = jnp.einsum("asd,asf->daf", slot_dy, activated, preferred_element_type=jnp.float32)
    shares = lax.psum_scatter(
        jnp.concatenate(
            [
                term_gate.reshape(lax.axis_size("dp") * share_width, block_width),
                term_up.reshape(lax.axis_size("dp") * share_width, block_width),
                term_down.reshape(lax.axis_size("dp") * share_width, block_width),
            ],
            axis=1,
        ).astype(jnp.bfloat16),
        "dp",
        scatter_dimension=0,
        tiled=True,
    ).astype(jnp.float32)
    share_rows = shares.shape[0]

    def unpack(which):
        return shares[:, which * block_width : (which + 1) * block_width].reshape(
            share_rows, local_count, hidden_units
        )

    gate_grad = unpack(0).transpose(1, 0, 2).astype(jnp.bfloat16)
    up_grad = unpack(1).transpose(1, 0, 2).astype(jnp.bfloat16)
    down_grad = unpack(2).transpose(1, 2, 0).astype(jnp.bfloat16)
    return (input_grad, gate_grad, up_grad, down_grad)


def solution(mesh):
    return jax.shard_map(
        local,
        mesh=mesh,
        in_specs=(
            P(("dp", "expert"), None),
            P(("dp", "expert"), None),
            P(("dp", "expert"), None),
            P(("dp", "expert"), None),
            P("expert", "dp", None),
            P("expert", "dp", None),
            P("expert", None, "dp"),
        ),
        out_specs=(
            P(("dp", "expert"), None),
            P("expert", "dp", None),
            P("expert", "dp", None),
            P("expert", None, "dp"),
        ),
        check_vma=False,
    )
```

profile of v0, /device:TPU:0, one launch (start us, length us, event | category | flops | bytes accessed | tf_op | source)
XLA Modules:
  0.0 274.2 jit_solution(3252684024728993636)
XLA Ops:
  7.2 0.7 all-gather.8.cloned.1.call-update
  8.0 0.7 all-gather.6.cloned.1.call-update
  8.7 0.7 broadcast_multiply_fusion
  9.4 0.8 copy.14
  10.1 0.1 eq.29
  10.2 0.1 eq.25
  10.4 0.1 copy.13
  10.5 0.1 mul.60
  10.6 1.1 reduce-window.6
  11.7 0.2 slice_reduce_fusion
  12.0 0.1 fusion.20
  12.1 2.4 scatter_custom_fusion
  14.6 0.1 broadcast_in_dim.41
  14.7 3.4 %gather_fusion.2 = bf16[576,2048]{1,0:T(8,128)(2,1)S(1)} fusion(bf16[128,2048]{1,0:T(8,128)(2,1)S(1)} %copy-done, s32[1024]{0:T(1024)S(1)} %get-tuple-element.19), kind=kCustom, calls=%fused_computation.2 | custom fusion | bytes 4720896 | tf_op jit(solution)/shard_map/gather | solution.py:29
  18.1 1.6 broadcast_select_fusion
  19.7 6.5 %all-to-all-start.1 = ((bf16[8,72,2048]{2,1,0:T(8,128)(2,1)}), bf16[8,72,2048]{2,1,0:T(8,128)(2,1)}, u32[]{:S(2)}, u32[]{:S(2)}) async-start(bf16[8,72,2048]{2,1,0:T(8,128)(2,1)} %broadcast_select_fusion), calls=%async_computation.1 | async-start | bytes 4718592 | tf_op jit(solution)/shard_map/all_to_all | solution.py:35
  26.3 0.1 copy.16
  26.4 0.1 reshape.168
  26.5 4.0 %gather_fusion = f32[576]{0:T(1024)S(1)} fusion(f32[512]{0:T(512)S(1)} %reshape.168, s32[1024]{0:T(1024)S(1)} %get-tuple-element.20), kind=kCustom, calls=%fused_computation | custom fusion | bytes 6912 | tf_op jit(solution)/shard_map/gather | solution.py:30
  30.4 0.1 mul.62
  30.5 3.4 %gather_fusion.1 = bf16[576,2048]{1,0:T(8,128)(2,1)S(1)} fusion(bf16[128,2048]{1,0:T(8,128)(2,1)S(1)} %copy-done.2, s32[1024]{0:T(1024)S(1)} %get-tuple-element.19), kind=kCustom, calls=%fused_computation.1 | custom fusion | bytes 4720896 | tf_op jit(solution)/shard_map/gather | solution.py:30
  33.9 2.0 fusion.1
  36.0 45.0 %all-to-all-done.1 = bf16[8,72,2048]{2,1,0:T(8,128)(2,1)} async-done(((bf16[8,72,2048]{2,1,0:T(8,128)(2,1)}), bf16[8,72,2048]{2,1,0:T(8,128)(2,1)}, u32[]{:S(2)}, u32[]{:S(2)}) %all-to-all-start.1) | async-done | bytes 2359328 | tf_op jit(solution)/shard_map/all_to_all | solution.py:35
  81.0 3.7 %all-to-all-start = ((bf16[8,72,2048]{2,1,0:T(8,128)(2,1)}), bf16[8,72,2048]{2,1,0:T(8,128)(2,1)S(1)}, u32[]{:S(2)}, u32[]{:S(2)}) async-start(bf16[8,72,2048]{2,1,0:T(8,128)(2,1)} %fusion.1), calls=%async_computation | async-start | bytes 4718592 | tf_op jit(solution)/shard_map/all_to_all | solution.py:36
  84.7 0.7 all-gather.4.cloned.1.call-update
  85.4 0.2 reduce-scatter.2.cloned.1.call-start
  85.7 5.8 %fusion.4 = f32[576,768]{1,0:T(8,128)} fusion(bf16[576,2048]{1,0:T(8,128)(2,1)} %bitcast.8, bf16[1,2048,768]{2,1,0:T(8,128)(2,1)} %all-gather.8.cloned.1.call-done), kind=kOutput, calls=%fused_computation.15 | convolution fusion | flops 1811939328 | bytes 7274496 | tf_op jit(solution)/shard_map/asd,adf->asf/dot_general | solution.py:46
  91.5 10.7 %all-gather.6.cloned.1.call-done = bf16[1,2048,768]{2,1,0:T(8,128)(2,1)} async-done(((bf16[1,512,768]{2,1,0:T(8,128)(2,1)}), bf16[1,2048,768]{2,1,0:T(8,128)(2,1)}) %all-gather.6.cloned.1.call-update) | async-done | bytes 3145744 | tf_op jit(solution)/shard_map/all_gather | solution.py:55
  102.1 5.8 %fusion.8 = f32[576,768]{1,0:T(8,128)} fusion(bf16[576,2048]{1,0:T(8,128)(2,1)} %bitcast.8, bf16[1,2048,768]{2,1,0:T(8,128)(2,1)} %all-gather.6.cloned.1.call-done), kind=kOutput, calls=%fused_computation.19 | convolution fusion | flops 1811939328 | bytes 7274496 | tf_op jit(solution)/shard_map/asd,adf->asf/dot_general | solution.py:52
  108.0 31.3 %all-to-all-done = bf16[8,72,2048]{2,1,0:T(8,128)(2,1)S(1)} async-done(((bf16[8,72,2048]{2,1,0:T(8,128)(2,1)}), bf16[8,72,2048]{2,1,0:T(8,128)(2,1)S(1)}, u32[]{:S(2)}, u32[]{:S(2)}) %all-to-all-start) | async-done | bytes 2359328 | tf_op jit(solution)/shard_map/all_to_all | solution.py:36
  139.3 6.2 %fusion.14 = bf16[2048,768]{0,1:T(8,128)(2,1)} fusion(bf16[576,2048]{1,0:T(8,128)(2,1)S(1)} %bitcast.74, f32[576,768]{1,0:T(8,128)} %fusion.8, f32[576,768]{1,0:T(8,128)} %fusion.4), kind=kOutput, calls=%fused_computation.25 | convolution fusion | flops 1816166400 | bytes 9043968 | tf_op jit(solution)/shard_map/asd,asf->daf/dot_general | solution.py:89
  145.5 2.2 all-gather.4.cloned.1.call-done
  147.7 5.4 %multiply_convert_fusion.1 = (bf16[576,768]{1,0:T(8,128)(2,1)S(1)}, bf16[576,768]{1,0:T(8,128)(2,1)S(1)}) fusion(f32[576,768]{1,0:T(8,128)} %fusion.4, f32[576,768]{1,0:T(8,128)} %fusion.8, bf16[576,2048]{1,0:T(8,128)(2,1)S(1)} %bitcast.75, bf16[1,768,2048]{2,1,0:T(8,128)(2,1)} %all-gather.4.cloned.1.call-done), kind=kOutput, calls=%fused_computation.28 | convolution fusion | flops 1817690112 | bytes 10813440 | tf_op jit(solution)/shard_map/asd,afd->asf/dot_general | solution.py:66
  153.2 5.2 %fusion.13 = bf16[2048,768]{0,1:T(8,128)(2,1)S(1)} fusion(bf16[576,768]{1,0:T(8,128)(2,1)S(1)} %get-tuple-element.12, bf16[576,2048]{1,0:T(8,128)(2,1)} %bitcast.8), kind=kOutput, calls=%fused_computation.24 | convolution fusion | flops 1813512192 | bytes 6389760 | tf_op jit(solution)/shard_map/asd,asf->daf/dot_general | solution.py:88
  158.4 4.7 %fusion.12 = bf16[2048,768]{0,1:T(8,128)(2,1)S(1)} fusion(bf16[576,768]{1,0:T(8,128)(2,1)S(1)} %get-tuple-element.13, bf16[576,2048]{1,0:T(8,128)(2,1)} %bitcast.8), kind=kOutput, calls=%fused_computation.23 | convolution fusion | flops 1813512192 | bytes 6389760 | tf_op jit(solution)/shard_map/asd,asf->daf/dot_general | solution.py:87
  163.1 4.5 %pad_maximum_fusion = bf16[2048,2304]{0,1:T(8,128)(2,1)} fusion(bf16[2048,768]{0,1:T(8,128)(2,1)S(1)} %copy-done.3, bf16[2048,768]{0,1:T(8,128)(2,1)S(1)} %fusion.13, bf16[2048,768]{0,1:T(8,128)(2,1)S(1)} %fusion.12), kind=kLoop, calls=%fused_computation.5 | loop fusion | flops 28311552 | bytes 18874368 | tf_op jit(solution)/shard_map/concatenate | solution.py:91
  167.6 1.1 copy-done.7
  168.8 4.1 %fusion.2 = f32[576,2048]{1,0:T(8,128)S(1)} fusion(bf16[576,768]{1,0:T(8,128)(2,1)S(1)} %copy-done.7, bf16[1,2048,768]{2,1,0:T(8,128)(2,1)} %all-gather.8.cloned.1.call-done), kind=kOutput, calls=%fused_computation.13 | convolution fusion | flops 1811939328 | bytes 8749056 | tf_op jit(solution)/shard_map/asf,adf->asd/dot_general | solution.py:72
  172.9 3.4 %add_convert_fusion = bf16[576,2048]{1,0:T(8,128)(2,1)} fusion(f32[576,2048]{1,0:T(8,128)S(1)} %fusion.2, bf16[576,768]{1,0:T(8,128)(2,1)S(1)} %copy-done.9, bf16[1,2048,768]{2,1,0:T(8,128)(2,1)S(1)} %copy-done.5), kind=kOutput, calls=%fused_computation.9 | convolution fusion | flops 1814298624 | bytes 11108352 | tf_op jit(solution)/shard_map/asf,adf->asd/dot_general | solution.py:73
  176.3 4.8 %all-to-all-start.2 = ((bf16[8,72,2048]{2,1,0:T(8,128)(2,1)}), bf16[8,72,2048]{2,1,0:T(8,128)(2,1)S(1)}, u32[]{:S(2)}, u32[]{:S(2)}) async-start(bf16[8,72,2048]{2,1,0:T(8,128)(2,1)} %bitcast.76), calls=%async_computation.2 | async-start | bytes 4718592 | tf_op jit(solution)/shard_map/all_to_all | solution.py:79
  181.1 54.6 %all-to-all-done.2 = bf16[8,72,2048]{2,1,0:T(8,128)(2,1)S(1)} async-done(((bf16[8,72,2048]{2,1,0:T(8,128)(2,1)}), bf16[8,72,2048]{2,1,0:T(8,128)(2,1)S(1)}, u32[]{:S(2)}, u32[]{:S(2)}) %all-to-all-start.2) | async-done | bytes 2359328 | tf_op jit(solution)/shard_map/all_to_all | solution.py:79
  235.8 3.3 %gather_fusion.3 = bf16[512,2048]{1,0:T(8,128)(2,1)} fusion(bf16[576,2048]{1,0:T(8,128)(2,1)S(1)} %bitcast.71, s32[1024]{0:T(1024)S(1)} %pad_clamp_fusion), kind=kCustom, calls=%fused_computation.3 | custom fusion | bytes 4196352 | tf_op jit(solution)/shard_map/gather | solution.py:80
  239.1 2.8 %gather.21 = bf16[128,4,2048]{2,1,0:T(4,128)(2,1)S(1)} reshape(bf16[512,2048]{1,0:T(8,128)(2,1)} %gather_fusion.3) | data formatting | bytes 4194304 | tf_op jit(solution)/shard_map/gather | solution.py:80
  241.9 4.0 %reduce_sum.25 = bf16[128,2048]{1,0:T(8,128)(2,1)} reduce(bf16[128,4,2048]{2,1,0:T(4,128)(2,1)S(1)} %gather.21, bf16[]{:T(256)} %constant.36.clone.1), dimensions={1}, to_apply=%region_4.5 | reduce | flops 786432 | bytes 2621442 | tf_op jit(solution)/shard_map/reduce_sum | solution.py:81
  245.9 16.8 %reduce-scatter.2.cloned.1.call-done = bf16[512,2304]{0,1:T(8,128)(2,1)} async-done(((bf16[2048,2304]{0,1:T(8,128)(2,1)}), bf16[512,2304]{0,1:T(8,128)(2,1)}) %reduce-scatter.2.cloned.1.call-update) | async-done | bytes 2359312 | tf_op jit(solution)/shard_map/reduce_scatter | solution.py:90
  262.7 2.7 slice_bitcast_fusion
  265.4 1.2 copy.18
  266.5 1.2 copy.17
  (33 shorter events, 0.3 us)
Async XLA Ops:
  7.2 7.5 %copy-start = (bf16[128,2048]{1,0:T(8,128)(2,1)S(1)}, bf16[128,2048]{1,0:T(8,128)(2,1)}, u32[]{:S(2)}) copy-start(bf16[128,2048]{1,0:T(8,128)(2,1)} %param.7) | copy-start | bytes 1572868
  7.2 78.5 %all-gather.8.cloned.1.call-start = ((), (), s32[]{:S(2)}) async-start(), calls=%async_computation.6 | async-start | bytes 3932160 | tf_op jit(solution)/shard_map/all_gather | solution.py:49
  7.9 94.2 %all-gather.6.cloned.1.call-start = ((), (), s32[]{:S(2)}) async-start(), calls=%async_computation.5 | async-start | bytes 3932160 | tf_op jit(solution)/shard_map/all_gather | solution.py:55
  19.7 6.5 %copy-start.4 = (f32[128,4]{0,1:T(4,128)S(1)}, f32[128,4]{0,1:T(4,128)}, u32[]{:S(2)}) copy-start(f32[128,4]{0,1:T(4,128)} %param.10) | copy-start | bytes 6148
  19.7 61.2 %all-to-all-start.1 = ((bf16[8,72,2048]{2,1,0:T(8,128)(2,1)}), bf16[8,72,2048]{2,1,0:T(8,128)(2,1)}, u32[]{:S(2)}, u32[]{:S(2)}) async-start(bf16[8,72,2048]{2,1,0:T(8,128)(2,1)} %broadcast_select_fusion), calls=%async_computation.1 | async-start | bytes 4718592 | tf_op jit(solution)/shard_map/all_to_all | solution.py:35
  26.2 4.3 %copy-start.2 = (bf16[128,2048]{1,0:T(8,128)(2,1)S(1)}, bf16[128,2048]{1,0:T(8,128)(2,1)}, u32[]{:S(2)}) copy-start(bf16[128,2048]{1,0:T(8,128)(2,1)} %param.8) | copy-start | bytes 1572868
  81.0 58.3 %all-to-all-start = ((bf16[8,72,2048]{2,1,0:T(8,128)(2,1)}), bf16[8,72,2048]{2,1,0:T(8,128)(2,1)S(1)}, u32[]{:S(2)}, u32[]{:S(2)}) async-start(bf16[8,72,2048]{2,1,0:T(8,128)(2,1)} %fusion.1), calls=%async_computation | async-start | bytes 4718592 | tf_op jit(solution)/shard_map/all_to_all | solution.py:36
  84.7 63.0 %all-gather.4.cloned.1.call-start = ((), (), s32[]{:S(2)}) async-start(), calls=%async_computation.4 | async-start | bytes 3932160 | tf_op jit(solution)/shard_map/all_gather | solution.py:61
  85.4 177.2 %reduce-scatter.2.cloned.1.call-start = ((), (), s32[]{:S(2)}) async-start(), calls=%async_computation.7 | async-start | bytes 11796480 | tf_op jit(solution)/shard_map/reduce_scatter | solution.py:90
  153.1 5.2 %copy-start.8 = (bf16[576,768]{1,0:T(8,128)(2,1)}, bf16[576,768]{1,0:T(8,128)(2,1)S(1)}, u32[]{:S(2)}) copy-start(bf16[576,768]{1,0:T(8,128)(2,1)S(1)} %get-tuple-element.12) | copy-start | bytes 2654212
  153.2 5.2 %copy-start.6 = (bf16[576,768]{1,0:T(8,128)(2,1)}, bf16[576,768]{1,0:T(8,128)(2,1)S(1)}, u32[]{:S(2)}) copy-start(bf16[576,768]{1,0:T(8,128)(2,1)S(1)} %get-tuple-element.13) | copy-start | bytes 2654212
  158.4 4.7 %copy-start.3 = (bf16[2048,768]{0,1:T(8,128)(2,1)S(1)}, bf16[2048,768]{0,1:T(8,128)(2,1)}, u32[]{:S(2)}) copy-start(bf16[2048,768]{0,1:T(8,128)(2,1)} %fusion.14) | copy-start | bytes 9437188
  167.6 1.2 copy-start.7
  168.8 4.1 %copy-start.5 = (bf16[1,2048,768]{2,1,0:T(8,128)(2,1)S(1)}, bf16[1,2048,768]{2,1,0:T(8,128)(2,1)}, u32[]{:S(2)}) copy-start(bf16[1,2048,768]{2,1,0:T(8,128)(2,1)} %all-gather.6.cloned.1.call-done) | copy-start | bytes 9437188
  168.8 4.1 %copy-start.9 = (bf16[576,768]{1,0:T(8,128)(2,1)S(1)}, bf16[576,768]{1,0:T(8,128)(2,1)}, u32[]{:S(2)}) copy-start(bf16[576,768]{1,0:T(8,128)(2,1)} %copy-done.8) | copy-start | bytes 2654212
  176.3 59.5 %all-to-all-start.2 = ((bf16[8,72,2048]{2,1,0:T(8,128)(2,1)}), bf16[8,72,2048]{2,1,0:T(8,128)(2,1)S(1)}, u32[]{:S(2)}, u32[]{:S(2)}) async-start(bf16[8,72,2048]{2,1,0:T(8,128)(2,1)} %bitcast.76), calls=%async_computation.2 | async-start | bytes 4718592 | tf_op jit(solution)/shard_map/all_to_all | solution.py:79
  262.7 5.0 %copy-start.1 = (bf16[128,2048]{1,0:T(8,128)(2,1)S(1)}, bf16[128,2048]{1,0:T(8,128)(2,1)}, u32[]{:S(2)}) copy-start(bf16[128,2048]{1,0:T(8,128)(2,1)} %param.7) | copy-start | bytes 1572868
Sparse Core Ops, SparseCore 0:
  9.8 46.5 all-gather.7
  58.3 43.8 all-gather.5
  104.0 43.6 all-gather.3
  167.7 94.8 reduce-scatter.1
where the time goes:
time: 275 us; the launch traced here: 274 us
  waiting for transfers between devices  163 us (59%)
  matrix products  40.7 us (15%)
  local copies, waits for them, and re-layouts  27.4 us (10%)
  starting transfers between devices  15.4 us (6%)
  other arithmetic  14.1 us (5%)
  between operations  14 us (5%)
    all_to_all x1, waiting for transfers between devices, local(): lax.all_to_all(send_back, 'expert', split_axis=0, concat_axis=0, tiled=True)  54.6 us
    all_to_all x1, waiting for transfers between devices, local(): lax.all_to_all(send_x, 'expert', split_axis=0, concat_axis=0, tiled=True)  45 us
    all_to_all x1, waiting for transfers between devices, local(): lax.all_to_all(send_dy, 'expert', split_axis=0, concat_axis=0, tiled=True)  31.3 us
    reduce_scatter x1, waiting for transfers between devices, local(): lax.psum_scatter(jnp.concatenate([term_gate.reshape(lax.axis_size('dp') *...  16.8 us
    all_gather x1, waiting for transfers between devices, local(): lax.all_gather(w_up, 'dp', axis=1, tiled=True)  10.7 us
    all_to_all x1, starting transfers between devices, local(): lax.all_to_all(send_x, 'expert', split_axis=0, concat_axis=0, tiled=True)  6.49 us
    dot_general x1, matrix products, local(): jnp.einsum('asd,asf->daf', slot_dy, activated, preferred_element_type=jnp...  6.23 us
    gather x2, local copies, waits for them, and re-layouts, local(): returned.reshape(expert_count * capacity, model_width)[slot_of]  6.13 us
  transfers between devices with their start and end apart: 7, of which 6 were waited for; matrix products, arithmetic and copies ran while one was open for 20% of the time, Pallas kernels for 0%

commit v1 on v0

--- a/solution.py
+++ b/solution.py
@@ -2,6 +2,29 @@
 import jax.numpy as jnp
 from jax import lax
 from jax.sharding import PartitionSpec as P
+
+
+def in_blocks(x, dim, size):
+    before, after = (x.shape[:dim], x.shape[dim + 1 :])
+    return jnp.moveaxis(x.reshape(*before, size, -1, *after), dim, 0)
+
+
+def joined_along(parts, dim):
+    dims = list(parts.shape[1:])
+    dims[dim] *= parts.shape[0]
+    return jnp.moveaxis(parts, 0, dim).reshape(dims)
+
+
+def rotated_exchange(x, axis, split_dim, concat_dim):
+    peers, position = (lax.axis_size(axis), lax.axis_index(axis))
+    blocks = in_blocks(x, split_dim, peers)
+    whole = blocks
+    for lap in range(1, peers):
+        target, source = ((position + lap) % peers, (position - lap) % peers)
+        sent = lax.dynamic_index_in_dim(blocks, target, 0)
+        other = lax.ppermute(sent, axis, [(i, (i + lap) % peers) for i in range(peers)])
+        whole = lax.dynamic_update_slice_in_dim(whole, other, source, axis=0)
+    return joined_along(whole, concat_dim)
 
 
 def local(tokens, out_grad, routes, gate_values, w_gate, w_up, w_down):
@@ -33,7 +56,7 @@
     send_dy = send_dy.reshape(expert_count, capacity, model_width)
     recv_x, recv_dy = (
         lax.all_to_all(send_x, "expert", split_axis=0, concat_axis=0, tiled=True),
-        lax.all_to_all(send_dy, "expert", split_axis=0, concat_axis=0, tiled=True),
+        rotated_exchange(send_dy, "expert", 0, 0),
     )
 
     def to_local(stacked):

time: 275 us -> 278 us (1.011)
  waiting for transfers between devices: 163 us -> 145 us
  starting transfers between devices: 15.4 us -> 31.4 us
  local copies, waits for them, and re-layouts: 27.4 us -> 36.6 us
  matrix products: 40.7 us -> 37.6 us
    ppermute x0 -> x7, waiting for transfers between devices: none -> 56.1 us  [rotated_exchange(): lax.ppermute(sent, axis, [(i, (i + lap) % peers) for i in range(peers)])]
    all_to_all x1, waiting for transfers between devices: 45 us -> 0.01 us  [local(): lax.all_to_all(send_x, 'expert', split_axis=0, concat_axis=0, tiled=True)]
    all_to_all x1 -> x0, waiting for transfers between devices: 31.3 us -> none  [local(): lax.all_to_all(send_dy, 'expert', split_axis=0, concat_axis=0, tiled=True)]
    ppermute x0 -> x7, starting transfers between devices: none -> 17.9 us  [rotated_exchange(): lax.ppermute(sent, axis, [(i, (i + lap) % peers) for i in range(peers)])]
    all_gather x1, waiting for transfers between devices: 2.22 us -> 14.2 us  [local(): lax.all_gather(w_down, 'dp', axis=2, tiled=True)]
    all_gather x1, waiting for transfers between devices: 10.7 us -> 0.01 us  [local(): lax.all_gather(w_up, 'dp', axis=1, tiled=True)]
    dynamic_update_slice x0 -> x6, local copies, waits for them, and re-layouts: none -> 4.4 us  [rotated_exchange(): whole = lax.dynamic_update_slice_in_dim(whole, other, source, axis=0)]
    all_to_all x1 -> x0, starting transfers between devices: 3.7 us -> none  [local(): lax.all_to_all(send_dy, 'expert', split_axis=0, concat_axis=0, tiled=True)]
  transfers between devices with their start and end apart: 7 -> 13, of which waited for: 6 -> 7; matrix products, arithmetic and copies ran while one was open for 20% -> 21% of each run, Pallas kernels for 0% -> 0%
where the time goes in v1:
time: 278 us; the launch traced here: 277 us
  waiting for transfers between devices  145 us (52%)
  matrix products  37.6 us (14%)
  local copies, waits for them, and re-layouts  36.6 us (13%)
  starting transfers between devices  31.4 us (11%)
  between operations  14.1 us (5%)
  other arithmetic  12.6 us (5%)
    ppermute x7, waiting for transfers between devices, rotated_exchange(): lax.ppermute(sent, axis, [(i, (i + lap) % peers) for i in range(peers)])  56.1 us
    all_to_all x1, waiting for transfers between devices, local(): lax.all_to_all(send_back, 'expert', split_axis=0, concat_axis=0, tiled=True)  54.6 us
    reduce_scatter x1, waiting for transfers between devices, local(): lax.psum_scatter(jnp.concatenate([term_gate.reshape(lax.axis_size('dp') *...  18.2 us
    ppermute x7, starting transfers between devices, rotated_exchange(): lax.ppermute(sent, axis, [(i, (i + lap) % peers) for i in range(peers)])  17.9 us
    all_gather x1, waiting for transfers between devices, local(): lax.all_gather(w_down, 'dp', axis=2, tiled=True)  14.2 us
    unnamed x32, local copies, waits for them, and re-layouts  6.99 us
    all_to_all x1, starting transfers between devices, local(): lax.all_to_all(send_back, 'expert', split_axis=0, concat_axis=0, tiled=True)  6.86 us
    all_to_all x1, starting transfers between devices, local(): lax.all_to_all(send_x, 'expert', split_axis=0, concat_axis=0, tiled=True)  6.49 us
  transfers between devices with their start and end apart: 13, of which 7 were waited for; matrix products, arithmetic and copies ran while one was open for 21% of the time, Pallas kernels for 0%

profile of v1, /device:TPU:0, one launch (start us, length us, event | category | flops | bytes accessed | tf_op | source)
XLA Modules:
  0.0 277.5 jit_solution(16528348888256378391)
XLA Ops:
  7.2 0.7 all-gather.8.cloned.1.call-update
  8.0 0.7 all-gather.6.cloned.1.call-update
  8.7 0.8 copy.14
  9.7 0.7 broadcast_multiply_fusion
  10.6 1.1 reduce-window.6
  12.1 2.4 scatter_custom_fusion
  14.7 3.4 %gather_fusion.2 = bf16[576,2048]{1,0:T(8,128)(2,1)S(1)} fusion(bf16[128,2048]{1,0:T(8,128)(2,1)S(1)} %copy-done, s32[1024]{0:T(1024)S(1)} %get-tuple-element.26), kind=kCustom, calls=%fused_computation.2 | custom fusion | bytes 4720896 | tf_op jit(solution)/shard_map/gather | solution.py:52
  18.1 1.7 broadcast_select_fusion
  19.8 6.5 %all-to-all-start = ((bf16[8,72,2048]{2,1,0:T(8,128)(2,1)}), bf16[8,72,2048]{2,1,0:T(8,128)(2,1)}, u32[]{:S(2)}, u32[]{:S(2)}) async-start(bf16[8,72,2048]{2,1,0:T(8,128)(2,1)} %broadcast_select_fusion), calls=%async_computation | async-start | bytes 4718592 | tf_op jit(solution)/shard_map/all_to_all | solution.py:58
  26.4 0.7 all-gather.4.cloned.1.call-update
  27.1 3.4 %gather_fusion.1 = bf16[576,2048]{1,0:T(8,128)(2,1)S(1)} fusion(bf16[128,2048]{1,0:T(8,128)(2,1)S(1)} %copy-done.2, s32[1024]{0:T(1024)S(1)} %get-tuple-element.26), kind=kCustom, calls=%fused_computation.1 | custom fusion | bytes 4720896 | tf_op jit(solution)/shard_map/gather | solution.py:53
  30.8 4.0 %gather_fusion = f32[576]{0:T(1024)S(1)} fusion(f32[512]{0:T(512)S(1)} %reshape.189, s32[1024]{0:T(1024)S(1)} %get-tuple-element.27), kind=kCustom, calls=%fused_computation | custom fusion | bytes 6912 | tf_op jit(solution)/shard_map/gather | solution.py:53
  35.4 1.4 copy-done.3
  37.4 35.1 %collective-permute-done = bf16[1,1,72,2048]{3,2,0,1:T(8,128)(2,1)S(1)} collective-permute-done((bf16[1,1,72,2048]{3,2,0,1:T(8,128)(2,1)S(1)}, bf16[1,1,72,2048]{3,2,0,1:T(8,128)(2,1)S(1)}, u32[]{:S(2)}, u32[]{:S(2)}) %collective-permute-start) | collective-permute-done | bytes 294944 | tf_op jit(solution)/shard_map/ppermute | solution.py:25
  72.5 2.4 constant_dynamic-slice_fusion
  74.9 9.8 %collective-permute-start.2 = (bf16[1,1,72,2048]{3,2,0,1:T(8,128)(2,1)S(1)}, bf16[1,1,72,2048]{3,2,0,1:T(8,128)(2,1)S(1)}, u32[]{:S(2)}, u32[]{:S(2)}) collective-permute-start(bf16[1,1,72,2048]{3,2,0,1:T(8,128)(2,1)S(1)} %get-tuple-element.21), channel_id=1, source_target_pairs={{0,3},{1,4},{2,5},{3,6},{4,7},{5,0},{6,1},{7,2},{8,11},{9,12},{10,... | collective-permute-start | bytes 884744 | tf_op jit(solution)/shard_map/ppermute | solution.py:25
  84.7 2.5 collective-permute-start.3
  87.2 2.2 collective-permute-start.4
  89.3 2.9 %collective-permute-start.5 = (bf16[1,1,72,2048]{3,2,0,1:T(8,128)(2,1)S(1)}, bf16[1,1,72,2048]{3,2,0,1:T(8,128)(2,1)S(1)}, u32[]{:S(2)}, u32[]{:S(2)}) collective-permute-start(bf16[1,1,72,2048]{3,2,0,1:T(8,128)(2,1)S(1)} %get-tuple-element.18), channel_id=1, source_target_pairs={{0,6},{1,7},{2,0},{3,1},{4,2},{5,3},{6,4},{7,5},{8,14},{9,15},{10,... | collective-permute-start | bytes 884744 | tf_op jit(solution)/shard_map/ppermute | solution.py:25
  92.3 0.7 constant_dynamic-update-slice_fusion.5
  93.0 19.0 %collective-permute-done.2 = bf16[1,1,72,2048]{3,2,0,1:T(8,128)(2,1)S(1)} collective-permute-done((bf16[1,1,72,2048]{3,2,0,1:T(8,128)(2,1)S(1)}, bf16[1,1,72,2048]{3,2,0,1:T(8,128)(2,1)S(1)}, u32[]{:S(2)}, u32[]{:S(2)}) %collective-permute-start.2) | collective-permute-done | bytes 294944 | tf_op jit(solution)/shard_map/ppermute | solution.py:25
  112.0 0.7 constant_dynamic-update-slice_fusion.4
  113.1 0.7 constant_dynamic-update-slice_fusion.3
  113.9 0.7 constant_dynamic-update-slice_fusion.2
  114.6 0.7 constant_dynamic-update-slice_fusion.1
  115.3 1.5 collective-permute-done.6
  116.9 0.7 constant_dynamic-update-slice_fusion
  117.6 5.8 %fusion.4 = f32[576,768]{1,0:T(8,128)} fusion(bf16[576,2048]{1,0:T(8,128)(2,1)} %bitcast.8, bf16[1,2048,768]{2,1,0:T(8,128)(2,1)} %all-gather.8.cloned.1.call-done), kind=kOutput, calls=%fused_computation.15 | convolution fusion | flops 1811939328 | bytes 7274496 | tf_op jit(solution)/shard_map/asd,adf->asf/dot_general | solution.py:69
  123.5 4.7 %fusion.8 = f32[576,768]{1,0:T(8,128)S(1)} fusion(bf16[576,2048]{1,0:T(8,128)(2,1)} %bitcast.8, bf16[1,2048,768]{2,1,0:T(8,128)(2,1)} %all-gather.6.cloned.1.call-done), kind=kOutput, calls=%fused_computation.19 | convolution fusion | flops 1811939328 | bytes 7274496 | tf_op jit(solution)/shard_map/asd,adf->asf/dot_general | solution.py:75
  128.2 1.2 copy-done.11
  129.4 4.1 %fusion.14 = bf16[2048,768]{0,1:T(8,128)(2,1)} fusion(bf16[576,2048]{1,0:T(8,128)(2,1)S(1)} %bitcast.73, f32[576,768]{1,0:T(8,128)S(1)} %fusion.8, f32[576,768]{1,0:T(8,128)S(1)} %copy-done.10), kind=kOutput, calls=%fused_computation.25 | convolution fusion | flops 1816166400 | bytes 9043968 | tf_op jit(solution)/shard_map/asd,asf->daf/dot_general | solution.py:112
  133.5 14.2 %all-gather.4.cloned.1.call-done = bf16[1,768,2048]{2,1,0:T(8,128)(2,1)} async-done(((bf16[1,768,512]{2,1,0:T(8,128)(2,1)}), bf16[1,768,2048]{2,1,0:T(8,128)(2,1)}) %all-gather.4.cloned.1.call-update) | async-done | bytes 3145744 | tf_op jit(solution)/shard_map/all_gather | solution.py:84
  147.8 5.4 %multiply_convert_fusion.1 = (bf16[576,768]{1,0:T(8,128)(2,1)S(1)}, bf16[576,768]{1,0:T(8,128)(2,1)S(1)}) fusion(f32[576,768]{1,0:T(8,128)} %fusion.4, f32[576,768]{1,0:T(8,128)} %copy-done.11, bf16[576,2048]{1,0:T(8,128)(2,1)S(1)} %bitcast.74, bf16[1,768,2048]{2,1,0:T(8,128)(2,1)} %all-gather.4.cloned.1.call-done), kind=kOutput, calls=%fused_computation.28 | convolution fusion | flops 1817690112 | bytes 10813440 | tf_op jit(solution)/shard_map/asd,afd->asf/dot_general | solution.py:89
  153.2 5.2 %fusion.13 = bf16[2048,768]{0,1:T(8,128)(2,1)S(1)} fusion(bf16[576,768]{1,0:T(8,128)(2,1)S(1)} %get-tuple-element.12, bf16[576,2048]{1,0:T(8,128)(2,1)} %bitcast.8), kind=kOutput, calls=%fused_computation.24 | convolution fusion | flops 1813512192 | bytes 6389760 | tf_op jit(solution)/shard_map/asd,asf->daf/dot_general | solution.py:111
  158.4 4.7 %fusion.12 = bf16[2048,768]{0,1:T(8,128)(2,1)S(1)} fusion(bf16[576,768]{1,0:T(8,128)(2,1)S(1)} %get-tuple-element.13, bf16[576,2048]{1,0:T(8,128)(2,1)} %bitcast.8), kind=kOutput, calls=%fused_computation.23 | convolution fusion | flops 1813512192 | bytes 6389760 | tf_op jit(solution)/shard_map/asd,asf->daf/dot_general | solution.py:110
  163.1 4.4 %pad_maximum_fusion = bf16[2048,2304]{0,1:T(8,128)(2,1)} fusion(bf16[2048,768]{0,1:T(8,128)(2,1)S(1)} %copy-done.5, bf16[2048,768]{0,1:T(8,128)(2,1)S(1)} %fusion.13, bf16[2048,768]{0,1:T(8,128)(2,1)S(1)} %fusion.12), kind=kLoop, calls=%fused_computation.5 | loop fusion | flops 28311552 | bytes 18874368 | tf_op jit(solution)/shard_map/concatenate | solution.py:114
  167.6 1.1 copy-done.9
  168.7 4.1 %fusion.2 = f32[576,2048]{1,0:T(8,128)S(1)} fusion(bf16[576,768]{1,0:T(8,128)(2,1)S(1)} %copy-done.9, bf16[1,2048,768]{2,1,0:T(8,128)(2,1)} %all-gather.8.cloned.1.call-done), kind=kOutput, calls=%fused_computation.13 | convolution fusion | flops 1811939328 | bytes 8749056 | tf_op jit(solution)/shard_map/asf,adf->asd/dot_general | solution.py:95
  172.8 3.5 %add_convert_fusion = bf16[576,2048]{1,0:T(8,128)(2,1)} fusion(f32[576,2048]{1,0:T(8,128)S(1)} %fusion.2, bf16[576,768]{1,0:T(8,128)(2,1)S(1)} %copy-done.13, bf16[1,2048,768]{2,1,0:T(8,128)(2,1)S(1)} %copy-done.7), kind=kOutput, calls=%fused_computation.9 | convolution fusion | flops 1814298624 | bytes 11108352 | tf_op jit(solution)/shard_map/asf,adf->asd/dot_general | solution.py:96
  176.4 6.9 %all-to-all-start.1 = ((bf16[8,72,2048]{2,1,0:T(8,128)(2,1)}), bf16[8,72,2048]{2,1,0:T(8,128)(2,1)S(1)}, u32[]{:S(2)}, u32[]{:S(2)}) async-start(bf16[8,72,2048]{2,1,0:T(8,128)(2,1)} %bitcast.75), calls=%async_computation.1 | async-start | bytes 4718592 | tf_op jit(solution)/shard_map/all_to_all | solution.py:102
  183.2 54.6 %all-to-all-done.1 = bf16[8,72,2048]{2,1,0:T(8,128)(2,1)S(1)} async-done(((bf16[8,72,2048]{2,1,0:T(8,128)(2,1)}), bf16[8,72,2048]{2,1,0:T(8,128)(2,1)S(1)}, u32[]{:S(2)}, u32[]{:S(2)}) %all-to-all-start.1) | async-done | bytes 2359328 | tf_op jit(solution)/shard_map/all_to_all | solution.py:102
  237.9 3.3 %gather_fusion.3 = bf16[512,2048]{1,0:T(8,128)(2,1)} fusion(bf16[576,2048]{1,0:T(8,128)(2,1)S(1)} %bitcast.70, s32[1024]{0:T(1024)S(1)} %pad_clamp_fusion), kind=kCustom, calls=%fused_computation.3 | custom fusion | bytes 4196352 | tf_op jit(solution)/shard_map/gather | solution.py:103
  241.1 2.7 gather.21
  243.9 3.9 %reduce_sum.25 = bf16[128,2048]{1,0:T(8,128)(2,1)} reduce(bf16[128,4,2048]{2,1,0:T(4,128)(2,1)S(1)} %gather.21, bf16[]{:T(256)} %constant.142.clone.1), dimensions={1}, to_apply=%region_4.5 | reduce | flops 786432 | bytes 2621442 | tf_op jit(solution)/shard_map/reduce_sum | solution.py:104
  247.7 18.2 %reduce-scatter.2.cloned.1.call-done = bf16[512,2304]{0,1:T(8,128)(2,1)} async-done(((bf16[2048,2304]{0,1:T(8,128)(2,1)}), bf16[512,2304]{0,1:T(8,128)(2,1)}) %reduce-scatter.2.cloned.1.call-update) | async-done | bytes 2359312 | tf_op jit(solution)/shard_map/reduce_scatter | solution.py:113
  265.9 2.7 slice_bitcast_fusion
  268.6 1.2 copy.17
  269.8 1.2 copy.18
  (61 shorter events, 3.0 us)
Async XLA Ops:
  7.2 7.5 %copy-start = (bf16[128,2048]{1,0:T(8,128)(2,1)S(1)}, bf16[128,2048]{1,0:T(8,128)(2,1)}, u32[]{:S(2)}) copy-start(bf16[128,2048]{1,0:T(8,128)(2,1)} %param.7) | copy-start | bytes 1572868
  7.2 110.4 %all-gather.8.cloned.1.call-start = ((), (), s32[]{:S(2)}) async-start(), calls=%async_computation.5 | async-start | bytes 3932160 | tf_op jit(solution)/shard_map/all_gather | solution.py:72
  7.9 115.5 %all-gather.6.cloned.1.call-start = ((), (), s32[]{:S(2)}) async-start(), calls=%async_computation.4 | async-start | bytes 3932160 | tf_op jit(solution)/shard_map/all_gather | solution.py:78
  19.8 7.3 %copy-start.2 = (bf16[128,2048]{1,0:T(8,128)(2,1)S(1)}, bf16[128,2048]{1,0:T(8,128)(2,1)}, u32[]{:S(2)}) copy-start(bf16[128,2048]{1,0:T(8,128)(2,1)} %param.8) | copy-start | bytes 1572868
  19.8 97.8 %all-to-all-start = ((bf16[8,72,2048]{2,1,0:T(8,128)(2,1)}), bf16[8,72,2048]{2,1,0:T(8,128)(2,1)}, u32[]{:S(2)}, u32[]{:S(2)}) async-start(bf16[8,72,2048]{2,1,0:T(8,128)(2,1)} %broadcast_select_fusion), calls=%async_computation | async-start | bytes 4718592 | tf_op jit(solution)/shard_map/all_to_all | solution.py:58
  26.3 121.5 %all-gather.4.cloned.1.call-start = ((), (), s32[]{:S(2)}) async-start(), calls=%async_computation.3 | async-start | bytes 3932160 | tf_op jit(solution)/shard_map/all_gather | solution.py:84
  27.0 238.9 %reduce-scatter.2.cloned.1.call-start = ((), (), s32[]{:S(2)}) async-start(), calls=%async_computation.6 | async-start | bytes 11796480 | tf_op jit(solution)/shard_map/reduce_scatter | solution.py:113
  27.1 3.4 %copy-start.6 = (f32[128,4]{0,1:T(4,128)S(1)}, f32[128,4]{0,1:T(4,128)}, u32[]{:S(2)}) copy-start(f32[128,4]{0,1:T(4,128)} %param.10) | copy-start | bytes 6148
  35.4 1.4 copy-start.3
  36.9 35.7 %collective-permute-start = (bf16[1,1,72,2048]{3,2,0,1:T(8,128)(2,1)S(1)}, bf16[1,1,72,2048]{3,2,0,1:T(8,128)(2,1)S(1)}, u32[]{:S(2)}, u32[]{:S(2)}) collective-permute-start(bf16[1,1,72,2048]{3,2,0,1:T(8,128)(2,1)S(1)} %constant_dynamic-slice_fusion.6), channel_id=1, source_target_pairs={{0,1},{1,2},{2,3},{3,4},{4,5},{5,6},{6,7},{7,0},{8,9},{9,10},{10,1... | collective-permute-start | bytes 884744 | tf_op jit(solution)/shard_map/ppermute | solution.py:25
  74.9 17.4 %collective-permute-start.1 = (bf16[1,1,72,2048]{3,2,0,1:T(8,128)(2,1)S(1)}, bf16[1,1,72,2048]{3,2,0,1:T(8,128)(2,1)S(1)}, u32[]{:S(2)}, u32[]{:S(2)}) collective-permute-start(bf16[1,1,72,2048]{3,2,0,1:T(8,128)(2,1)S(1)} %get-tuple-element.22), channel_id=1, source_target_pairs={{0,2},{1,3},{2,4},{3,5},{4,6},{5,7},{6,0},{7,1},{8,10},{9,11},{10,... | collective-permute-start | bytes 884744 | tf_op jit(solution)/shard_map/ppermute | solution.py:25
  74.9 37.1 %collective-permute-start.2 = (bf16[1,1,72,2048]{3,2,0,1:T(8,128)(2,1)S(1)}, bf16[1,1,72,2048]{3,2,0,1:T(8,128)(2,1)S(1)}, u32[]{:S(2)}, u32[]{:S(2)}) collective-permute-start(bf16[1,1,72,2048]{3,2,0,1:T(8,128)(2,1)S(1)} %get-tuple-element.21), channel_id=1, source_target_pairs={{0,3},{1,4},{2,5},{3,6},{4,7},{5,0},{6,1},{7,2},{8,11},{9,12},{10,... | collective-permute-start | bytes 884744 | tf_op jit(solution)/shard_map/ppermute | solution.py:25
  84.7 28.4 %collective-permute-start.3 = (bf16[1,1,72,2048]{3,2,0,1:T(8,128)(2,1)S(1)}, bf16[1,1,72,2048]{3,2,0,1:T(8,128)(2,1)S(1)}, u32[]{:S(2)}, u32[]{:S(2)}) collective-permute-start(bf16[1,1,72,2048]{3,2,0,1:T(8,128)(2,1)S(1)} %get-tuple-element.20), channel_id=1, source_target_pairs={{0,4},{1,5},{2,6},{3,7},{4,0},{5,1},{6,2},{7,3},{8,12},{9,13},{10,... | collective-permute-start | bytes 884744 | tf_op jit(solution)/shard_map/ppermute | solution.py:25
  87.2 26.7 %collective-permute-start.4 = (bf16[1,1,72,2048]{3,2,0,1:T(8,128)(2,1)S(1)}, bf16[1,1,72,2048]{3,2,0,1:T(8,128)(2,1)S(1)}, u32[]{:S(2)}, u32[]{:S(2)}) collective-permute-start(bf16[1,1,72,2048]{3,2,0,1:T(8,128)(2,1)S(1)} %get-tuple-element.19), channel_id=1, source_target_pairs={{0,5},{1,6},{2,7},{3,0},{4,1},{5,2},{6,3},{7,4},{8,13},{9,14},{10,... | collective-permute-start | bytes 884744 | tf_op jit(solution)/shard_map/ppermute | solution.py:25
  89.3 25.3 %collective-permute-start.5 = (bf16[1,1,72,2048]{3,2,0,1:T(8,128)(2,1)S(1)}, bf16[1,1,72,2048]{3,2,0,1:T(8,128)(2,1)S(1)}, u32[]{:S(2)}, u32[]{:S(2)}) collective-permute-start(bf16[1,1,72,2048]{3,2,0,1:T(8,128)(2,1)S(1)} %get-tuple-element.18), channel_id=1, source_target_pairs={{0,6},{1,7},{2,0},{3,1},{4,2},{5,3},{6,4},{7,5},{8,14},{9,15},{10,... | collective-permute-start | bytes 884744 | tf_op jit(solution)/shard_map/ppermute | solution.py:25
  92.3 24.6 %collective-permute-start.6 = (bf16[1,1,72,2048]{3,2,0,1:T(8,128)(2,1)S(1)}, bf16[1,1,72,2048]{3,2,0,1:T(8,128)(2,1)S(1)}, u32[]{:S(2)}, u32[]{:S(2)}) collective-permute-start(bf16[1,1,72,2048]{3,2,0,1:T(8,128)(2,1)S(1)} %get-tuple-element.17), channel_id=1, source_target_pairs={{0,7},{1,0},{2,1},{3,2},{4,3},{5,4},{6,5},{7,6},{8,15},{9,8},{10,9... | collective-permute-start | bytes 884744 | tf_op jit(solution)/shard_map/ppermute | solution.py:25
  123.4 6.0 %copy-start.4 = (bf16[8,1,72,2048]{3,2,0,1:T(8,128)(2,1)S(1)}, bf16[8,1,72,2048]{3,2,0,1:T(8,128)(2,1)}, u32[]{:S(2)}) copy-start(bf16[8,1,72,2048]{3,2,0,1:T(8,128)(2,1)} %constant_dynamic-update-slice_fusion) | copy-start | bytes 7077892
  123.5 6.0 %copy-start.10 = (f32[576,768]{1,0:T(8,128)S(1)}, f32[576,768]{1,0:T(8,128)}, u32[]{:S(2)}) copy-start(f32[576,768]{1,0:T(8,128)} %fusion.4) | copy-start | bytes 5308420
  128.2 1.2 copy-start.11
  153.2 5.2 %copy-start.12 = (bf16[576,768]{1,0:T(8,128)(2,1)}, bf16[576,768]{1,0:T(8,128)(2,1)S(1)}, u32[]{:S(2)}) copy-start(bf16[576,768]{1,0:T(8,128)(2,1)S(1)} %get-tuple-element.12) | copy-start | bytes 2654212
  153.2 5.2 %copy-start.8 = (bf16[576,768]{1,0:T(8,128)(2,1)}, bf16[576,768]{1,0:T(8,128)(2,1)S(1)}, u32[]{:S(2)}) copy-start(bf16[576,768]{1,0:T(8,128)(2,1)S(1)} %get-tuple-element.13) | copy-start | bytes 2654212
  158.4 4.7 %copy-start.5 = (bf16[2048,768]{0,1:T(8,128)(2,1)S(1)}, bf16[2048,768]{0,1:T(8,128)(2,1)}, u32[]{:S(2)}) copy-start(bf16[2048,768]{0,1:T(8,128)(2,1)} %fusion.14) | copy-start | bytes 9437188
  167.6 1.2 copy-start.9
  168.7 4.1 %copy-start.7 = (bf16[1,2048,768]{2,1,0:T(8,128)(2,1)S(1)}, bf16[1,2048,768]{2,1,0:T(8,128)(2,1)}, u32[]{:S(2)}) copy-start(bf16[1,2048,768]{2,1,0:T(8,128)(2,1)} %all-gather.6.cloned.1.call-done) | copy-start | bytes 9437188
  168.7 4.1 %copy-start.13 = (bf16[576,768]{1,0:T(8,128)(2,1)S(1)}, bf16[576,768]{1,0:T(8,128)(2,1)}, u32[]{:S(2)}) copy-start(bf16[576,768]{1,0:T(8,128)(2,1)} %copy-done.12) | copy-start | bytes 2654212
  176.4 61.5 %all-to-all-start.1 = ((bf16[8,72,2048]{2,1,0:T(8,128)(2,1)}), bf16[8,72,2048]{2,1,0:T(8,128)(2,1)S(1)}, u32[]{:S(2)}, u32[]{:S(2)}) async-start(bf16[8,72,2048]{2,1,0:T(8,128)(2,1)} %bitcast.75), calls=%async_computation.1 | async-start | bytes 4718592 | tf_op jit(solution)/shard_map/all_to_all | solution.py:102
  265.9 5.0 %copy-start.1 = (bf16[128,2048]{1,0:T(8,128)(2,1)S(1)}, bf16[128,2048]{1,0:T(8,128)(2,1)}, u32[]{:S(2)}) copy-start(bf16[128,2048]{1,0:T(8,128)(2,1)} %param.7) | copy-start | bytes 1572868
Sparse Core Ops, SparseCore 0:
  9.8 46.6 all-gather.7
  58.3 43.8 all-gather.5
  104.0 43.6 all-gather.3
  167.7 98.1 reduce-scatter.1
